TPU v7x, 512 devices: a whole 4x4x16 slice. The times are simulated.
512 devices in a mesh: occ: 16 (over x_hi, y, core), vir: 32 (over z, x_lo).
Axes of the slice: x: 4 (x_hi: 2, x_lo: 2; x = x_hi * 2 + x_lo), y: 4, z: 16, core: 2. Of those that a mesh axis runs over, the one named last changes fastest.
Arguments:
- orbitals: bfloat16 [16, 8192, 4096], P('occ', 'vir'), may hold values from -0.75 to 0.75
- eps_occ: bfloat16 [16], P('occ'), may hold values from -2.5 to -0.5
- eps_vir: bfloat16 [8192], P('vir'), may hold values from 0.5 to 3
Outputs:
- density: bfloat16 [16, 8192, 4096], P('occ', 'vir')
All inputs are finite; a program needn't handle non-finite values.
Results may differ from a plain program's by a relative error of at most 0.0047.
Values may be sent and summed in bfloat16 or wider, within the bound.
No kernel may reach another device: no remote copies, remote signals or barrier semaphores. Data moves between devices by JAX's collectives and lax.ppermute only.
A program may use at most 64 MiB of HBM per device.

v0:
```python
import jax
import jax.numpy as jnp
from jax import lax
from jax.sharding import PartitionSpec as P

BATCH_DEV = 8
REACH = 1


def shifted_2(block, axis, distance):
    devices = range(lax.axis_size(axis))
    route = [((i - distance) % len(devices), i) for i in devices]
    return lax.ppermute(block, axis, route)


def pair_energies(eps_occ, occ_stack, eps_vir, batch_energy):
    own_energy = eps_occ.astype(jnp.float32)
    others = occ_stack.astype(jnp.float32)
    vir_energy = eps_vir.astype(jnp.float32)
    batch_virt = batch_energy.astype(jnp.float32)
    return (
        vir_energy[None, :, None, None, None]
        + batch_virt[None, None, None, None, :]
        - own_energy[:, None, None, None, None]
        - others[None, None, :, :, None]
    )


def shards(orbitals, eps_occ, eps_vir):
    occ_dev, vir_dev, aux_width = orbitals.shape
    block_count = 2 * REACH + 1
    offsets = list(range(-REACH, REACH + 1))
    resident = orbitals.reshape(occ_dev * vir_dev, aux_width)
    energies = []
    slices = []
    for offset in offsets:
        if offset == 0:
            slices.append(orbitals)
            energies.append(eps_occ)
        else:
            shifted, shifted_energy = shifted_2((orbitals, eps_occ), "occ", -offset)
            slices.append(shifted)
            energies.append(shifted_energy)
    stacked = jnp.stack([one_slice[:, :BATCH_DEV, :] for one_slice in slices])
    row_sets, batch_energy = (
        lax.all_gather(stacked, "vir", axis=2, tiled=True),
        lax.all_gather(eps_vir[:BATCH_DEV], "vir", axis=0, tiled=True),
    )
    batch_width = row_sets.shape[2]
    coulomb = jnp.einsum(
        "rp,cp->rc",
        resident,
        row_sets.reshape(block_count * occ_dev * batch_width, aux_width),
        preferred_element_type=jnp.float32,
    )
    coulomb = coulomb.reshape(occ_dev, vir_dev, block_count, occ_dev, batch_width)
    exchange = jnp.einsum(
        "kjap,ibp->iakjb", jnp.stack(slices), row_sets[REACH], preferred_element_type=jnp.float32
    )
    denominator = pair_energies(eps_occ, jnp.stack(energies), eps_vir, batch_energy)
    amplitude = ((2.0 * coulomb - exchange) / denominator).astype(jnp.bfloat16)
    density = jnp.dot(
        amplitude.reshape(occ_dev * vir_dev, block_count * occ_dev * batch_width),
        row_sets.reshape(block_count * occ_dev * batch_width, aux_width),
        preferred_element_type=jnp.float32,
    )
    return density.reshape(occ_dev, vir_dev, aux_width).astype(jnp.bfloat16)


def solution(mesh):
    return jax.shard_map(
        shards,
        mesh=mesh,
        in_specs=(P("occ", "vir", None), P("occ"), P("vir")),
        out_specs=P("occ", "vir", None),
        check_vma=False,
    )
```

profile of v0, /device:TPU:8, one launch (start us, length us, event | category | flops | bytes accessed | tf_op | source)
XLA Modules:
  0.0 225.0 jit_solution(18331232845301097830)
XLA Ops:
  6.5 0.0 all-gather.2.cloned.1.call-start
  6.5 1.9 collective-permute-start.1
  8.5 2.4 %collective-permute-start = (bf16[1,256,4096]{2,1,0:T(8,128)(2,1)}, bf16[1,256,4096]{2,1,0:T(8,128)(2,1)S(1)}, u32[]{:S(2)}, u32[]{:S(2)}) collective-permute-start(bf16[1,256,4096]{2,1,0:T(8,128)(2,1)} %param.3), channel_id=1, source_target_pairs={{480,0},{0,32},{32,64},{64,96},{96,128},{128,160},{160,192},{192,2... | collective-permute-start | bytes 6291464 | tf_op jit(solution)/shard_map/ppermute | solution.py:13
  10.9 0.8 slice_bitcast_fusion.12
  11.7 20.6 %collective-permute-done.1 = bf16[1,256,4096]{2,1,0:T(8,128)(2,1)S(1)} collective-permute-done((bf16[1,256,4096]{2,1,0:T(8,128)(2,1)}, bf16[1,256,4096]{2,1,0:T(8,128)(2,1)S(1)}, u32[]{:S(2)}, u32[]{:S(2)}) %collective-permute-start.1) | collective-permute-done | bytes 2097184 | tf_op jit(solution)/shard_map/ppermute | solution.py:13
  32.3 7.9 %collective-permute-done = bf16[1,256,4096]{2,1,0:T(8,128)(2,1)S(1)} collective-permute-done((bf16[1,256,4096]{2,1,0:T(8,128)(2,1)}, bf16[1,256,4096]{2,1,0:T(8,128)(2,1)S(1)}, u32[]{:S(2)}, u32[]{:S(2)}) %collective-permute-start) | collective-permute-done | bytes 2097184 | tf_op jit(solution)/shard_map/ppermute | solution.py:13
  40.2 0.0 copy-start.2
  40.2 1.3 copy-done.2
  41.5 0.7 pad_maximum_fusion
  42.2 0.0 all-gather.2.cloned.1.call-update
  42.2 1.9 collective-permute-start.2
  44.2 3.6 %collective-permute-start.3 = (bf16[1]{0:T(256)(128)(2,1)}, bf16[1]{0:T(256)(128)(2,1)}, u32[]{:S(2)}, u32[]{:S(2)}) collective-permute-start(bf16[1]{0:T(256)(128)(2,1)} %param.4), channel_id=1, source_target_pairs={{32,0},{64,32},{96,64},{128,96},{160,128},{192,160},{224,192},{256... | collective-permute-start | bytes 14 | tf_op jit(solution)/shard_map/ppermute | solution.py:13
  48.5 0.7 convert_element_type.25
  49.2 1.3 dynamic-slice
  51.2 0.9 dynamic-update-slice
  52.1 67.1 %all-reduce = bf16[256]{0:T(256)(128)(2,1)S(1)} all-reduce(bf16[256]{0:T(256)(128)(2,1)S(1)} %dynamic-update-slice), channel_id=1, replica_groups=mesh['occ'=16,'vir'=32] {'vir'}, use_global_device_ids=true, to_apply=%add | all-reduce | flops 256 | bytes 1024
  119.1 0.1 add_subtract_fusion
  119.3 0.0 collective-permute-done.2
  119.3 0.0 collective-permute-done.3
  119.3 1.4 maximum_convert_fusion
  120.7 86.0 %all-gather.2.cloned.1.call-done = bf16[3,1,256,4096]{3,2,1,0:T(8,128)(2,1)} async-done(((bf16[3,1,8,4096]{3,2,1,0:T(8,128)(2,1)}), bf16[3,1,256,4096]{3,2,1,0:T(8,128)(2,1)}) %all-gather.2.cloned.1.call-update) | async-done | bytes 6291472 | tf_op jit(solution)/shard_map/all_gather | solution.py:46
  206.6 0.0 copy-start
  206.7 0.0 copy-start.1
  206.7 0.0 copy-start.3
  206.7 5.4 %fusion.9 = f32[768,256]{1,0:T(8,128)S(1)} fusion(bf16[768,4096]{1,0:T(8,128)(2,1)} %bitcast.65, bf16[1,256,4096]{2,1,0:T(8,128)(2,1)} %param.3), kind=kOutput, calls=%fused_computation.12 | convolution fusion | flops 1610809344 | bytes 9175040 | tf_op jit(solution)/shard_map/rp,cp->rc/dot_general | solution.py:50
  212.0 0.0 copy-done
  212.1 0.4 copy-done.1
  212.5 0.6 copy-done.3
  213.1 1.9 fusion.14
  214.9 3.2 %fusion.5 = bf16[1,256,4096]{2,1,0:T(8,128)(2,1)} fusion(bf16[256,768]{0,1:T(8,128)(2,1)S(1)} %bitcast.67, bf16[768,4096]{1,0:T(8,128)(2,1)S(1)} %bitcast.66), kind=kOutput, calls=%fused_computation.7 | convolution fusion | flops 1611661312 | bytes 8781824 | tf_op jit(solution)/shard_map/dot_general | solution.py:62
  (4 shorter events, 0.0 us)
Async XLA Ops:
  6.5 200.1 %all-gather.2.cloned.1.call-start = ((), (), s32[]{:S(2)}) async-start(), calls=%async_computation | async-start | bytes 6488064 | tf_op jit(solution)/shard_map/all_gather | solution.py:46
  6.5 25.8 %collective-permute-start.1 = (bf16[1,256,4096]{2,1,0:T(8,128)(2,1)}, bf16[1,256,4096]{2,1,0:T(8,128)(2,1)S(1)}, u32[]{:S(2)}, u32[]{:S(2)}) collective-permute-start(bf16[1,256,4096]{2,1,0:T(8,128)(2,1)} %param.3), channel_id=1, source_target_pairs={{32,0},{64,32},{96,64},{128,96},{160,128},{192,160},{224,192},{256... | collective-permute-start | bytes 6291464 | tf_op jit(solution)/shard_map/ppermute | solution.py:13
  8.5 31.7 %collective-permute-start = (bf16[1,256,4096]{2,1,0:T(8,128)(2,1)}, bf16[1,256,4096]{2,1,0:T(8,128)(2,1)S(1)}, u32[]{:S(2)}, u32[]{:S(2)}) collective-permute-start(bf16[1,256,4096]{2,1,0:T(8,128)(2,1)} %param.3), channel_id=1, source_target_pairs={{480,0},{0,32},{32,64},{64,96},{96,128},{128,160},{160,192},{192,2... | collective-permute-start | bytes 6291464 | tf_op jit(solution)/shard_map/ppermute | solution.py:13
  40.2 1.3 copy-start.2
  42.2 77.0 %collective-permute-start.2 = (bf16[1]{0:T(256)(128)(2,1)}, bf16[1]{0:T(256)(128)(2,1)}, u32[]{:S(2)}, u32[]{:S(2)}) collective-permute-start(bf16[1]{0:T(256)(128)(2,1)} %param.4), channel_id=1, source_target_pairs={{480,0},{0,32},{32,64},{64,96},{96,128},{128,160},{160,192},{192,2... | collective-permute-start | bytes 14 | tf_op jit(solution)/shard_map/ppermute | solution.py:13
  44.2 75.1 %collective-permute-start.3 = (bf16[1]{0:T(256)(128)(2,1)}, bf16[1]{0:T(256)(128)(2,1)}, u32[]{:S(2)}, u32[]{:S(2)}) collective-permute-start(bf16[1]{0:T(256)(128)(2,1)} %param.4), channel_id=1, source_target_pairs={{32,0},{64,32},{96,64},{128,96},{160,128},{192,160},{224,192},{256... | collective-permute-start | bytes 14 | tf_op jit(solution)/shard_map/ppermute | solution.py:13
  206.6 5.4 %copy-start = (bf16[3,1,256,4096]{3,2,1,0:T(8,128)(2,1)S(1)}, bf16[3,1,256,4096]{3,2,1,0:T(8,128)(2,1)}, u32[]{:S(2)}) copy-start(bf16[3,1,256,4096]{3,2,1,0:T(8,128)(2,1)} %all-gather.2.cloned.1.call-done) | copy-start | bytes 18874372
  206.7 5.8 %copy-start.1 = (bf16[1,256,4096]{2,1,0:T(8,128)(2,1)S(1)}, bf16[1,256,4096]{2,1,0:T(8,128)(2,1)}, u32[]{:S(2)}) copy-start(bf16[1,256,4096]{2,1,0:T(8,128)(2,1)} %param.3) | copy-start | bytes 6291460
  206.7 6.4 %copy-start.3 = (bf16[1,256,4096]{2,1,0:T(8,128)(2,1)S(1)}, bf16[1,256,4096]{2,1,0:T(8,128)(2,1)}, u32[]{:S(2)}) copy-start(bf16[1,256,4096]{2,1,0:T(8,128)(2,1)} %copy-done.2) | copy-start | bytes 6291460
Sparse Core Ops, SparseCore 0:
  42.4 164.2 all-gather.1
where the time goes:
time: 225 us
  waiting for transfers between devices  114 us (51%)
  blocking collectives  67.1 us (30%)
  between operations  14.9 us (7%)
  matrix products  10.5 us (5%)
  starting transfers between devices  9.89 us (4%)
  local copies, waits for them, and re-layouts  5.4 us (2%)
  other arithmetic  2.84 us (1%)
    all_gather x1, waiting for transfers between devices, shards(): lax.all_gather(stacked, 'vir', axis=2, tiled=True)  86 us
    unnamed x1, blocking collectives  67.1 us
    ppermute x4, waiting for transfers between devices, shifted_2(): return lax.ppermute(block, axis, route)  28.5 us
    ppermute x4, starting transfers between devices, shifted_2(): return lax.ppermute(block, axis, route)  9.89 us
    dot_general x1, matrix products, shards(): jnp.einsum('rp,cp->rc', resident, row_sets.reshape(block_count * occ_dev...  5.38 us
    unnamed x11, local copies, waits for them, and re-layouts  4.54 us
  transfers between devices with their start and end apart: 5, of which 3 were waited for; matrix products, arithmetic and copies ran while one was open for 2% of the time, Pallas kernels for 0%

commit v1 on v0

--- a/solution.py
+++ b/solution.py
@@ -43,7 +43,9 @@
             energies.append(shifted_energy)
     stacked = jnp.stack([one_slice[:, :BATCH_DEV, :] for one_slice in slices])
     row_sets, batch_energy = (
-        lax.all_gather(stacked, "vir", axis=2, tiled=True),
+        jnp.concatenate(
+            lax.all_to_all(jnp.stack([stacked] * lax.axis_size("vir")), "vir", 0, 0), axis=2
+        ),
         lax.all_gather(eps_vir[:BATCH_DEV], "vir", axis=0, tiled=True),
     )
     batch_width = row_sets.shape[2]

time: 225 us -> 389 us (1.73)
  blocking collectives: 67.1 us -> 316 us
  waiting for transfers between devices: 114 us -> 27.2 us
  between operations: 14.9 us -> 1.53 us
  starting transfers between devices: 9.89 us -> 22.4 us
  local copies, waits for them, and re-layouts: 5.4 us -> 12.3 us
    unnamed x1, blocking collectives: 67.1 us -> 316 us
    all_gather x1 -> x0, waiting for transfers between devices: 86 us -> none  [shards(): lax.all_gather(stacked, 'vir', axis=2, tiled=True)]
    all_to_all x0 -> x1, starting transfers between devices: none -> 12.5 us  [shards(): lax.all_to_all(jnp.stack([stacked] * lax.axis_size('vir')), 'vir', 0, 0)]
  transfers between devices with their start and end apart: 5 -> 5, of which waited for: 3 -> 2; matrix products, arithmetic and copies ran while one was open for 2% -> 1% of each run, Pallas kernels for 0% -> 0%
where the time goes in v1:
time: 389 us; the launch traced here: 388 us
  blocking collectives  316 us (81%)
  waiting for transfers between devices  27.2 us (7%)
  starting transfers between devices  22.4 us (6%)
  local copies, waits for them, and re-layouts  12.3 us (3%)
  matrix products  6.9 us (2%)
    unnamed x1, blocking collectives  316 us
    ppermute x4, waiting for transfers between devices, shifted_2(): return lax.ppermute(block, axis, route)  27.2 us
    all_to_all x1, starting transfers between devices, shards(): lax.all_to_all(jnp.stack([stacked] * lax.axis_size('vir')), 'vir', 0, 0)  12.5 us
    ppermute x4, starting transfers between devices, shifted_2(): return lax.ppermute(block, axis, route)  9.89 us
  transfers between devices with their start and end apart: 5, of which 2 were waited for; matrix products, arithmetic and copies ran while one was open for 1% of the time, Pallas kernels for 0%

profile of v1, /device:TPU:8, one launch (start us, length us, event | category | flops | bytes accessed | tf_op | source)
XLA Modules:
  0.0 388.1 jit_solution(12408199539615198185)
XLA Ops:
  0.0 1.9 collective-permute-start.1
  1.9 2.4 collective-permute-start
  4.3 0.8 slice_bitcast_fusion.12
  5.2 20.6 %collective-permute-done.1 = bf16[1,256,4096]{2,1,0:T(8,128)(2,1)S(1)} collective-permute-done((bf16[1,256,4096]{2,1,0:T(8,128)(2,1)}, bf16[1,256,4096]{2,1,0:T(8,128)(2,1)S(1)}, u32[]{:S(2)}, u32[]{:S(2)}) %collective-permute-start.1) | collective-permute-done | bytes 2097184 | tf_op jit(solution)/shard_map/ppermute | solution.py:13
  25.8 0.0 copy-start.1
  25.8 1.3 copy-done.1
  27.1 6.6 %collective-permute-done = bf16[1,256,4096]{2,1,0:T(8,128)(2,1)S(1)} collective-permute-done((bf16[1,256,4096]{2,1,0:T(8,128)(2,1)}, bf16[1,256,4096]{2,1,0:T(8,128)(2,1)S(1)}, u32[]{:S(2)}, u32[]{:S(2)}) %collective-permute-start) | collective-permute-done | bytes 2097184 | tf_op jit(solution)/shard_map/ppermute | solution.py:13
  33.6 0.0 copy-start.3
  33.7 1.3 copy-done.3
  35.0 3.4 stack.27
  38.4 0.0 copy-start.5
  38.4 12.5 %all-to-all-start = ((bf16[32,3,1,8,4096]{4,3,2,1,0:T(8,128)(2,1)}), bf16[32,3,1,8,4096]{4,3,2,1,0:T(8,128)(2,1)}, u32[]{:S(2)}, u32[]{:S(2)}) async-start(bf16[32,3,1,8,4096]{4,3,2,1,0:T(8,128)(2,1)} %stack.27), calls=%async_computation | async-start | bytes 12582912 | tf_op jit(solution)/shard_map/all_to_all | solution.py:47
  50.9 1.9 collective-permute-start.2
  52.9 3.6 collective-permute-start.3
  57.2 0.0 copy-done.5
  57.2 1.3 dynamic-slice
  59.3 0.2 dynamic-update-slice
  59.5 316.4 %all-reduce = bf16[256]{0:T(256)(128)(2,1)S(1)} all-reduce(bf16[256]{0:T(256)(128)(2,1)S(1)} %dynamic-update-slice), channel_id=1, replica_groups=mesh['occ'=16,'vir'=32] {'vir'}, use_global_device_ids=true, to_apply=%add | all-reduce | flops 256 | bytes 1024
  375.9 0.1 add_subtract_fusion
  376.0 0.0 collective-permute-done.2
  376.0 0.0 collective-permute-done.3
  376.0 1.4 maximum_convert_fusion
  377.4 0.0 copy-start
  377.4 0.0 all-to-all-done
  377.4 3.4 copy.10
  380.8 0.0 copy-start.2
  380.8 0.0 copy-start.4
  380.8 0.0 copy-done
  380.8 1.8 fusion.9
  382.7 0.0 copy-done.2
  382.7 0.4 copy-done.4
  383.0 1.8 fusion.14
  384.9 3.2 fusion.5
  (6 shorter events, 0.0 us)
Async XLA Ops:
  0.0 25.8 %collective-permute-start.1 = (bf16[1,256,4096]{2,1,0:T(8,128)(2,1)}, bf16[1,256,4096]{2,1,0:T(8,128)(2,1)S(1)}, u32[]{:S(2)}, u32[]{:S(2)}) collective-permute-start(bf16[1,256,4096]{2,1,0:T(8,128)(2,1)} %param.3), channel_id=1, source_target_pairs={{32,0},{64,32},{96,64},{128,96},{160,128},{192,160},{224,192},{256... | collective-permute-start | bytes 6291464 | tf_op jit(solution)/shard_map/ppermute | solution.py:13
  1.9 31.7 %collective-permute-start = (bf16[1,256,4096]{2,1,0:T(8,128)(2,1)}, bf16[1,256,4096]{2,1,0:T(8,128)(2,1)S(1)}, u32[]{:S(2)}, u32[]{:S(2)}) collective-permute-start(bf16[1,256,4096]{2,1,0:T(8,128)(2,1)} %param.3), channel_id=1, source_target_pairs={{480,0},{0,32},{32,64},{64,96},{96,128},{128,160},{160,192},{192,2... | collective-permute-start | bytes 6291464 | tf_op jit(solution)/shard_map/ppermute | solution.py:13
  25.8 1.3 copy-start.1
  33.6 1.3 copy-start.3
  38.4 18.8 %copy-start.5 = (bf16[256]{0:T(256)(128)(2,1)S(1)}, bf16[256]{0:T(256)(128)(2,1)}, u32[]{:S(2)}) copy-start(bf16[256]{0:T(256)(128)(2,1)} %param.5) | copy-start | bytes 1540
  38.4 339.0 %all-to-all-start = ((bf16[32,3,1,8,4096]{4,3,2,1,0:T(8,128)(2,1)}), bf16[32,3,1,8,4096]{4,3,2,1,0:T(8,128)(2,1)}, u32[]{:S(2)}, u32[]{:S(2)}) async-start(bf16[32,3,1,8,4096]{4,3,2,1,0:T(8,128)(2,1)} %stack.27), calls=%async_computation | async-start | bytes 12582912 | tf_op jit(solution)/shard_map/all_to_all | solution.py:47
  50.9 325.1 %collective-permute-start.2 = (bf16[1]{0:T(256)(128)(2,1)}, bf16[1]{0:T(256)(128)(2,1)}, u32[]{:S(2)}, u32[]{:S(2)}) collective-permute-start(bf16[1]{0:T(256)(128)(2,1)} %param.4), channel_id=1, source_target_pairs={{480,0},{0,32},{32,64},{64,96},{96,128},{128,160},{160,192},{192,2... | collective-permute-start | bytes 14 | tf_op jit(solution)/shard_map/ppermute | solution.py:13
  52.9 323.2 %collective-permute-start.3 = (bf16[1]{0:T(256)(128)(2,1)}, bf16[1]{0:T(256)(128)(2,1)}, u32[]{:S(2)}, u32[]{:S(2)}) collective-permute-start(bf16[1]{0:T(256)(128)(2,1)} %param.4), channel_id=1, source_target_pairs={{32,0},{64,32},{96,64},{128,96},{160,128},{192,160},{224,192},{256... | collective-permute-start | bytes 14 | tf_op jit(solution)/shard_map/ppermute | solution.py:13
  377.4 3.4 copy-start
  380.8 1.9 copy-start.2
  380.8 2.2 copy-start.4
